TPU v7x, 32 devices: a whole 2x2x4 slice. The times are simulated.
32 devices in a mesh: groups: 2 (over y), ctx: 8 (over z, x), head: 2 (over core).
Axes of the slice: x: 2, y: 2, z: 4, core: 2. Of those that a mesh axis runs over, the one named last changes fastest.
Arguments:
- keys_values: bfloat16 [2, 8192, 1024], P(None, ('groups', 'ctx'), 'head'), parts along dimension 1, may hold values from -6 to 6
- span_order: int32 [32], P('groups'), parts along dimension 0, may hold values from 0 to 15, as said below
- page_table: int32 [64], P('groups'), parts along dimension 0, may hold values from 0 to 31, as said below
Outputs:
- paged_cache: bfloat16 [2, 64, 128, 1024], P(None, ('groups', 'ctx', 'head')), parts along dimension 1
There are 2 independent parts, one for each index of `groups`. A program takes and returns all parts, laid end to end along the dimension named above; each array names one. Nothing has to cross between parts.
Inputs may be any that keep to these rules, and one draw needn't show every extreme that they name: `span_order`: blocks 2 c and 2 c + 1 hold two spans whose numbers add to 15; every span is held once. A permutation of the slots in which page p goes to a slot of p // 2, that is page_table[p] // 2 == p // 2.
All inputs are finite; a program needn't handle non-finite values.
Results may differ from a plain program's by a relative error of at most 0.001.
Values may be sent and summed in bfloat16 or wider, within the bound.
No kernel may reach another device: no remote copies, remote signals or barrier semaphores. Data moves between devices by JAX's collectives and lax.ppermute only.
A program may use at most 64 MiB of HBM per device.

v0:
```python
import jax
import jax.numpy as jnp
from jax import lax
from jax.sharding import PartitionSpec as P

PAGE = 128


def per_device(keys_values, span_order, page_table):
    tok_rows = keys_values.shape[1]
    span_len = tok_rows // 2
    half_width = keys_values.shape[2]
    ctx_size = lax.axis_size("ctx")
    ctx_index = lax.axis_index("ctx")
    head_index = lax.axis_index("head")
    spread_size = ctx_size * lax.axis_size("head")
    piece_rows = span_len // spread_size
    blocks = keys_values.reshape(2, 2, spread_size, piece_rows, half_width)
    spread = lax.all_to_all(blocks, ("ctx", "head"), split_axis=2, concat_axis=2, tiled=True)
    spread = spread.reshape(2, 2, ctx_size, 2, piece_rows, half_width)
    spread = spread.transpose(0, 2, 1, 4, 3, 5).reshape(2, 2 * ctx_size, piece_rows, 2 * half_width)
    holder = (
        jnp.zeros((2 * ctx_size,), jnp.int32)
        .at[span_order]
        .set(jnp.arange(2 * ctx_size, dtype=jnp.int32))
    )
    routed = jnp.take(spread, holder, axis=1)
    routed = lax.all_to_all(routed, ("ctx", "head"), split_axis=1, concat_axis=1, tiled=True)
    span_rows = routed.reshape(2, span_len, 2 * half_width)
    decode_index = ctx_index * 2 + head_index
    per_span = span_len // PAGE
    local_slots = (
        lax.dynamic_slice_in_dim(page_table, decode_index * per_span, per_span)
        - decode_index * per_span
    )
    slot_order = (
        jnp.zeros((per_span,), jnp.int32).at[local_slots].set(jnp.arange(per_span, dtype=jnp.int32))
    )
    page_blocks = span_rows.reshape(2, per_span, PAGE, 2 * half_width)
    paged_cache = jnp.take(page_blocks, slot_order, axis=1)
    return paged_cache


def solution(mesh):
    in_specs = (P(None, ("groups", "ctx"), "head"), P("groups"), P("groups"))
    out_specs = P(None, ("groups", "ctx", "head"), None, None)
    return jax.shard_map(
        per_device, mesh=mesh, in_specs=in_specs, out_specs=out_specs, check_vma=False
    )
```

profile of v0, /device:TPU:9, one launch (start us, length us, event | category | flops | bytes accessed | tf_op | source)
XLA Modules:
  0.0 69.1 jit_solution(5052322920109994542)
XLA Ops:
  0.0 2.3 %copy.13 = bf16[2,2,16,16,512]{4,3,1,0,2:T(8,128)(2,1)} copy(bf16[2,2,16,16,512]{4,3,2,1,0:T(8,128)(2,1)} %bitcast.11) | data formatting | bytes 2097152 | tf_op jit(solution)/shard_map/reshape | solution.py:18
  2.3 0.0 copy-start.1
  2.3 6.7 %all-to-all-start = ((bf16[2,2,16,16,512]{4,3,1,0,2:T(8,128)(2,1)}), bf16[2,2,16,16,512]{4,3,1,0,2:T(8,128)(2,1)S(1)}, u32[]{:S(2)}, u32[]{:S(2)}) async-start(bf16[2,2,16,16,512]{4,3,1,0,2:T(8,128)(2,1)} %copy.13), calls=%async_computation | async-start | bytes 2097152 | tf_op jit(solution)/shard_map/all_to_all | solution.py:19
  9.0 0.0 copy-done.1
  9.0 0.6 scatter_custom_fusion.1
  9.7 24.2 %all-to-all-done = bf16[2,2,16,16,512]{4,3,1,0,2:T(8,128)(2,1)S(1)} async-done(((bf16[2,2,16,16,512]{4,3,1,0,2:T(8,128)(2,1)}), bf16[2,2,16,16,512]{4,3,1,0,2:T(8,128)(2,1)S(1)}, u32[]{:S(2)}, u32[]{:S(2)}) %all-to-all-start) | async-done | bytes 1048608 | tf_op jit(solution)/shard_map/all_to_all | solution.py:19
  33.9 1.1 %copy.15 = bf16[2,8,2,16,2,512]{5,4,3,2,1,0:T(2,128)(2,1)S(1)} copy(bf16[2,8,2,16,2,512]{5,3,2,0,4,1:T(8,128)(2,1)S(1)} %bitcast.10) | data formatting | bytes 2097152 | tf_op jit(solution)/shard_map/transpose | solution.py:21
  35.0 0.8 %reshape.21 = bf16[2,16,16,1024]{3,2,1,0:T(8,128)(2,1)S(1)} reshape(bf16[2,8,2,16,2,512]{5,4,3,2,1,0:T(2,128)(2,1)S(1)} %copy.15) | data formatting | bytes 2097152 | tf_op jit(solution)/shard_map/reshape | solution.py:21
  35.8 0.6 gather_fusion
  36.4 1.1 %select_bitcast_fusion.1 = bf16[2,16,16,1024]{3,2,0,1:T(8,128)(2,1)} fusion(bf16[16,2,16,1024]{3,2,1,0:T(8,128)(2,1)S(1)} %gather_fusion, pred[16]{0:T(512)(128)(4,1)S(1)} %compare_and_fusion), kind=kLoop, calls=%fused_computation.5 | loop fusion | flops 524288 | bytes 2097168 | tf_op jit(solution)/shard_map/jit(_take)/select_n | solution.py:27
  37.5 4.8 %all-to-all-start.1 = ((bf16[2,16,16,1024]{3,2,0,1:T(8,128)(2,1)}), bf16[2,16,16,1024]{3,2,0,1:T(8,128)(2,1)S(1)}, u32[]{:S(2)}, u32[]{:S(2)}) async-start(bf16[2,16,16,1024]{3,2,0,1:T(8,128)(2,1)} %select_bitcast_fusion.1), calls=%async_computation.1 | async-start | bytes 2097152 | tf_op jit(solution)/shard_map/all_to_all | solution.py:28
  42.3 0.0 copy-start
  42.3 0.6 copy-done
  42.9 0.1 compare_select_fusion.3
  43.0 0.6 scatter_custom_fusion
  43.6 23.6 %all-to-all-done.1 = bf16[2,16,16,1024]{3,2,0,1:T(8,128)(2,1)S(1)} async-done(((bf16[2,16,16,1024]{3,2,0,1:T(8,128)(2,1)}), bf16[2,16,16,1024]{3,2,0,1:T(8,128)(2,1)S(1)}, u32[]{:S(2)}, u32[]{:S(2)}) %all-to-all-start.1) | async-done | bytes 1048608 | tf_op jit(solution)/shard_map/all_to_all | solution.py:28
  67.2 0.1 copy.16
  67.3 0.6 gather_fusion.1
  67.9 0.2 select_bitcast_fusion
  68.1 1.0 %copy.17 = bf16[2,2,128,1024]{3,2,1,0:T(8,128)(2,1)} copy(bf16[2,2,128,1024]{3,2,0,1:T(8,128)(2,1)S(1)} %select_bitcast_fusion) | data formatting | bytes 2097152 | tf_op jit(solution)/shard_map/jit(_take)/select_n | solution.py:40
  (9 shorter events, 0.0 us)
Async XLA Ops:
  2.3 6.7 %copy-start.1 = (s32[16]{0:T(128)S(1)}, s32[16]{0:T(128)}, u32[]{:S(2)}) copy-start(s32[16]{0:T(128)} %param.4) | copy-start | bytes 196
  2.3 31.6 %all-to-all-start = ((bf16[2,2,16,16,512]{4,3,1,0,2:T(8,128)(2,1)}), bf16[2,2,16,16,512]{4,3,1,0,2:T(8,128)(2,1)S(1)}, u32[]{:S(2)}, u32[]{:S(2)}) async-start(bf16[2,2,16,16,512]{4,3,1,0,2:T(8,128)(2,1)} %copy.13), calls=%async_computation | async-start | bytes 2097152 | tf_op jit(solution)/shard_map/all_to_all | solution.py:19
  37.5 29.7 %all-to-all-start.1 = ((bf16[2,16,16,1024]{3,2,0,1:T(8,128)(2,1)}), bf16[2,16,16,1024]{3,2,0,1:T(8,128)(2,1)S(1)}, u32[]{:S(2)}, u32[]{:S(2)}) async-start(bf16[2,16,16,1024]{3,2,0,1:T(8,128)(2,1)} %select_bitcast_fusion.1), calls=%async_computation.1 | async-start | bytes 2097152 | tf_op jit(solution)/shard_map/all_to_all | solution.py:28
  42.3 0.7 copy-start
where the time goes:
time: 69.5 us; the launch traced here: 69.1 us
  waiting for transfers between devices  47.8 us (69%)
  starting transfers between devices  11.4 us (16%)
  local copies, waits for them, and re-layouts  8.36 us (12%)
  other arithmetic  1.42 us (2%)
    all_to_all x1, waiting for transfers between devices, per_device(): lax.all_to_all(blocks, ('ctx', 'head'), split_axis=2, concat_axis=2, tile...  24.2 us
    all_to_all x1, waiting for transfers between devices, per_device(): lax.all_to_all(routed, ('ctx', 'head'), split_axis=1, concat_axis=1, tile...  23.6 us
    all_to_all x1, starting transfers between devices, per_device(): lax.all_to_all(blocks, ('ctx', 'head'), split_axis=2, concat_axis=2, tile...  6.68 us
    all_to_all x1, starting transfers between devices, per_device(): lax.all_to_all(routed, ('ctx', 'head'), split_axis=1, concat_axis=1, tile...  4.76 us
    reshape x1, local copies, waits for them, and re-layouts, per_device(): blocks = keys_values.reshape(2, 2, spread_size, piece_rows, half_width)  2.29 us
  transfers between devices with their start and end apart: 2, of which 2 were waited for; matrix products, arithmetic and copies ran while one was open for 2% of the time, Pallas kernels for 0%

commit v1 on v0

v1 whole, which is shorter than its diff:
```python
import jax
import jax.numpy as jnp
from jax import lax
from jax.sharding import PartitionSpec as P

PAGE = 128


def per_device(keys_values, span_order, page_table):
    tok_rows = keys_values.shape[1]
    width = keys_values.shape[2]
    span_len = tok_rows // 2
    per_span = span_len // PAGE
    ctx_index = lax.axis_index("ctx")
    spans = lax.axis_size("ctx") * lax.axis_size("head")
    half = spans // 2
    piece = span_len // half

    first_span = lax.dynamic_index_in_dim(span_order, 2 * ctx_index, keepdims=False)
    swap = first_span >= half
    blocks = keys_values.reshape(2, 2, half, piece, width)
    low = jnp.where(swap, blocks[:, 1], blocks[:, 0])
    high = jnp.where(swap, blocks[:, 0], blocks[:, 1])
    spread = jnp.stack([low, high], axis=0).transpose(0, 2, 1, 3, 4)
    spread = spread.reshape(spans, 2, piece, width)
    spread = lax.all_to_all(spread, ("ctx", "head"), split_axis=0, concat_axis=0, tiled=True)

    device = 2 * ctx_index + lax.axis_index("head")
    base = (device // half) * half
    wanted = base + jnp.arange(half, dtype=jnp.int32)
    chips = jnp.arange(spans, dtype=jnp.int32) // 2
    holder = jnp.sum(jnp.where(span_order[None, :] == wanted[:, None], chips[None, :], 0), axis=1)
    spread = spread.reshape(half, 2, 2, piece, width)
    routed = jnp.take(spread, holder, axis=0, mode="clip")
    groups = [list(range(half)), list(range(half, spans))]
    routed = lax.all_to_all(
        routed, ("ctx", "head"), split_axis=0, concat_axis=0, tiled=True, axis_index_groups=groups
    )
    rows = routed.transpose(2, 0, 3, 1, 4).reshape(2, per_span, PAGE, 2 * width)
    slots = lax.dynamic_slice_in_dim(page_table, device * per_span, per_span) - device * per_span
    order = jnp.sum(
        jnp.where(
            slots[None, :] == jnp.arange(per_span, dtype=jnp.int32)[:, None],
            jnp.arange(per_span, dtype=jnp.int32)[None, :],
            0,
        ),
        axis=1,
    )
    return jnp.take(rows, order, axis=1, mode="clip")


def solution(mesh):
    in_specs = (P(None, ("groups", "ctx"), "head"), P("groups"), P("groups"))
    out_specs = P(None, ("groups", "ctx", "head"), None, None)
    return jax.shard_map(
        per_device, mesh=mesh, in_specs=in_specs, out_specs=out_specs, check_vma=False
    )
```

time: 69.5 us -> 60.4 us (0.87)
  the two profiles are of different devices: /device:TPU:9 before, /device:TPU:0 now
where the time goes in v1:
time: 60.4 us; the launch traced here: 60.1 us
  waiting for transfers between devices  35.6 us (59%)
  starting transfers between devices  13.2 us (22%)
  local copies, waits for them, and re-layouts  8.75 us (14%)
  other arithmetic  1.82 us (3%)
  between operations  0.76 us (1%)
    all_to_all x1, waiting for transfers between devices, per_device(): lax.all_to_all(spread, ('ctx', 'head'), split_axis=0, concat_axis=0, tile...  22 us
    all_to_all x1, waiting for transfers between devices, per_device(): lax.all_to_all(routed, ('ctx', 'head'), split_axis=0, concat_axis=0, tile...  13.6 us
    all_to_all x1, starting transfers between devices, per_device(): lax.all_to_all(spread, ('ctx', 'head'), split_axis=0, concat_axis=0, tile...  7.39 us
    all_to_all x1, starting transfers between devices, per_device(): lax.all_to_all(routed, ('ctx', 'head'), split_axis=0, concat_axis=0, tile...  5.79 us
    gather x2, local copies, waits for them, and re-layouts, per_device(): return jnp.take(rows, order, axis=1, mode='clip')  1.65 us
    gather x1, local copies, waits for them, and re-layouts, per_device(): routed = jnp.take(spread, holder, axis=0, mode='clip')  1.58 us
    dynamic_slice x1, local copies, waits for them, and re-layouts, per_device(): lax.dynamic_index_in_dim(span_order, 2 * ctx_index, keepdims=False)  1.33 us
    unnamed x6, local copies, waits for them, and re-layouts  1.29 us
  transfers between devices with their start and end apart: 2, of which 2 were waited for; matrix products, arithmetic and copies ran while one was open for 1% of the time, Pallas kernels for 0%

profile of v1, /device:TPU:0, one launch (start us, length us, event | category | flops | bytes accessed | tf_op | source)
XLA Modules:
  0.0 60.1 jit_solution(13353969726236854624)
XLA Ops:
  0.0 0.0 copy-start
  0.0 1.3 %dynamic_slice.7 = s32[1]{0:T(128)} dynamic-slice(s32[16]{0:T(128)} %param.4, s32[]{:T(128)S(6)} %select_n.61), dynamic_slice_sizes={1} | dynamic-slice | bytes 12 | tf_op jit(solution)/shard_map/jit(dynamic_index_in_dim)/dynamic_slice | solution.py:19
  2.0 1.3 %fusion = bf16[1,2,8,32,512]{4,3,2,1,0:T(8,128)(2,1)S(1)} fusion(pred[]{:T(512)} %bitcast, bf16[2,2,8,32,512]{4,3,2,1,0:T(8,128)(2,1)} %bitcast.26), kind=kLoop, calls=%fused_computation.4 | loop fusion | flops 262144 | bytes 1572865 | tf_op jit(solution)/shard_map/jit(_where)/select_n | solution.py:23
  3.2 0.0 copy-done
  3.3 0.1 fusion.1
  3.3 0.1 maximum_bitcast_fusion
  3.4 1.0 %copy.20 = bf16[2,8,2,32,512]{4,3,2,1,0:T(8,128)(2,1)} copy(bf16[2,8,2,32,512]{4,3,1,2,0:T(8,128)(2,1)S(1)} %maximum_bitcast_fusion) | data formatting | bytes 2097152 | tf_op jit(solution)/shard_map/transpose | solution.py:24
  4.5 7.4 %all-to-all-start = ((bf16[16,2,32,512]{3,2,1,0:T(8,128)(2,1)}), bf16[16,2,32,512]{3,2,1,0:T(8,128)(2,1)S(1)}, u32[]{:S(2)}, u32[]{:S(2)}) async-start(bf16[16,2,32,512]{3,2,1,0:T(8,128)(2,1)} %bitcast.8), calls=%async_computation | async-start | bytes 2097152 | tf_op jit(solution)/shard_map/all_to_all | solution.py:26
  11.9 0.0 copy-start.1
  11.9 0.6 %copy-done.1 = s32[16]{0:T(128)S(1)} copy-done((s32[16]{0:T(128)S(1)}, s32[16]{0:T(128)}, u32[]{:S(2)}) %copy-start.1) | copy-done | bytes 88
  12.6 0.2 select_reduce_fusion
  12.8 22.0 %all-to-all-done = bf16[16,2,32,512]{3,2,1,0:T(8,128)(2,1)S(1)} async-done(((bf16[16,2,32,512]{3,2,1,0:T(8,128)(2,1)}), bf16[16,2,32,512]{3,2,1,0:T(8,128)(2,1)S(1)}, u32[]{:S(2)}, u32[]{:S(2)}) %all-to-all-start) | async-done | bytes 1048608 | tf_op jit(solution)/shard_map/all_to_all | solution.py:26
  34.8 1.6 %gather_fusion = bf16[8,2,2,32,512]{4,3,2,1,0:T(8,128)(2,1)} fusion(bf16[8,2,2,32,512]{4,3,2,1,0:T(8,128)(2,1)S(1)} %bitcast.24, s32[1024]{0:T(1024)S(1)} %pad_clamp_fusion.1), kind=kCustom, calls=%fused_computation | custom fusion | bytes 2097184 | tf_op jit(solution)/shard_map/jit(_take)/gather | solution.py:34
  36.3 5.8 %all-to-all-start.1 = ((bf16[8,2,2,32,512]{4,3,2,1,0:T(8,128)(2,1)}), bf16[8,2,2,32,512]{4,3,2,1,0:T(8,128)(2,1)S(1)}, u32[]{:S(2)}, u32[]{:S(2)}) async-start(bf16[8,2,2,32,512]{4,3,2,1,0:T(8,128)(2,1)} %gather_fusion), calls=%async_computation.1 | async-start | bytes 2097152 | tf_op jit(solution)/shard_map/all_to_all | solution.py:36
  42.1 0.0 copy-start.2
  42.1 0.7 %copy-done.2 = s32[32]{0:T(128)S(1)} copy-done((s32[32]{0:T(128)S(1)}, s32[32]{0:T(128)}, u32[]{:S(2)}) %copy-start.2) | copy-done | bytes 152
  42.8 0.1 dynamic-slice_subtract_fusion
  42.9 0.1 fusion.2
  43.0 13.6 %all-to-all-done.1 = bf16[8,2,2,32,512]{4,3,2,1,0:T(8,128)(2,1)S(1)} async-done(((bf16[8,2,2,32,512]{4,3,2,1,0:T(8,128)(2,1)}), bf16[8,2,2,32,512]{4,3,2,1,0:T(8,128)(2,1)S(1)}, u32[]{:S(2)}, u32[]{:S(2)}) %all-to-all-start.1) | async-done | bytes 1048608 | tf_op jit(solution)/shard_map/all_to_all | solution.py:36
  56.6 1.1 %copy.21 = bf16[2,8,32,2,512]{4,3,2,1,0:T(2,128)(2,1)S(1)} copy(bf16[2,8,32,2,512]{4,2,0,3,1:T(8,128)(2,1)S(1)} %bitcast.28) | data formatting | bytes 2097152 | tf_op jit(solution)/shard_map/transpose | solution.py:39
  57.7 0.8 %reshape.74 = bf16[2,2,128,1024]{3,2,1,0:T(8,128)(2,1)S(1)} reshape(bf16[2,8,32,2,512]{4,3,2,1,0:T(2,128)(2,1)S(1)} %copy.21) | data formatting | bytes 2097152 | tf_op jit(solution)/shard_map/reshape | solution.py:39
  58.5 0.6 %gather_fusion.1 = bf16[2,2,128,1024]{3,2,1,0:T(8,128)(2,1)S(1)} fusion(bf16[2,2,128,1024]{3,2,1,0:T(8,128)(2,1)S(1)} %reshape.74, s32[1024]{0:T(1024)S(1)} %pad_clamp_fusion), kind=kCustom, calls=%fused_computation.1 | custom fusion | bytes 2097160 | tf_op jit(solution)/shard_map/jit(_take)/gather | solution.py:49
  59.1 1.0 %copy.22 = bf16[2,2,128,1024]{3,2,1,0:T(8,128)(2,1)} copy(bf16[2,2,128,1024]{3,2,0,1:T(8,128)(2,1)S(1)} %bitcast.25) | data formatting | bytes 2097152 | tf_op jit(solution)/shard_map/jit(_take)/gather | solution.py:49
  (4 shorter events, 0.0 us)
Async XLA Ops:
  0.0 3.3 %copy-start = (bf16[2,512,512]{2,1,0:T(8,128)(2,1)S(1)}, bf16[2,512,512]{2,1,0:T(8,128)(2,1)}, u32[]{:S(2)}) copy-start(bf16[2,512,512]{2,1,0:T(8,128)(2,1)} %param.3) | copy-start | bytes 3145732
  4.5 30.3 %all-to-all-start = ((bf16[16,2,32,512]{3,2,1,0:T(8,128)(2,1)}), bf16[16,2,32,512]{3,2,1,0:T(8,128)(2,1)S(1)}, u32[]{:S(2)}, u32[]{:S(2)}) async-start(bf16[16,2,32,512]{3,2,1,0:T(8,128)(2,1)} %bitcast.8), calls=%async_computation | async-start | bytes 2097152 | tf_op jit(solution)/shard_map/all_to_all | solution.py:26
  11.9 0.7 %copy-start.1 = (s32[16]{0:T(128)S(1)}, s32[16]{0:T(128)}, u32[]{:S(2)}) copy-start(s32[16]{0:T(128)} %param.4) | copy-start | bytes 196
  36.3 20.3 %all-to-all-start.1 = ((bf16[8,2,2,32,512]{4,3,2,1,0:T(8,128)(2,1)}), bf16[8,2,2,32,512]{4,3,2,1,0:T(8,128)(2,1)S(1)}, u32[]{:S(2)}, u32[]{:S(2)}) async-start(bf16[8,2,2,32,512]{4,3,2,1,0:T(8,128)(2,1)} %gather_fusion), calls=%async_computation.1 | async-start | bytes 2097152 | tf_op jit(solution)/shard_map/all_to_all | solution.py:36
  42.1 0.7 %copy-start.2 = (s32[32]{0:T(128)S(1)}, s32[32]{0:T(128)}, u32[]{:S(2)}) copy-start(s32[32]{0:T(128)} %param.5) | copy-start | bytes 388
